TPU v7x, 32 devices: a whole 2x2x4 slice. The times are simulated.
32 devices in a mesh: seq: 4 (over y, x), feat: 8 (over z, core).
Axes of the slice: x: 2, y: 2, z: 4, core: 2. Of those that a mesh axis runs over, the one named last changes fastest.
Arguments:
- queries: bfloat16 [3840, 16, 128], P('seq'), may hold values from -32 to 32
- key_vectors: bfloat16 [3840, 16, 128], P('seq'), may hold values from -32 to 32
- values: bfloat16 [3840, 16, 128], P('seq'), may hold values from -6 to 6
- projections: bfloat16 [16, 4096, 128], P(None, 'feat'), may hold values from -4 to 4
Outputs:
- attended: bfloat16 [3840, 16, 128], P('seq', 'feat')
All inputs are finite; a program needn't handle non-finite values.
Results may differ from a plain program's by a relative error of at most 0.012.
Values may be sent and summed in bfloat16 or wider, within the bound.
A program may use at most 128 MiB of HBM per device.

v0:
```python
import jax
import jax.numpy as jnp
from jax import lax
from jax.sharding import PartitionSpec as P

E = 128


def key_exponents(key_vectors, directions, scaling):
    key_dash = (
        jnp.einsum("the,hme->thm", key_vectors, directions, preferred_element_type=jnp.float32)
        * scaling
    )
    key_diag = jnp.sum(jnp.square(key_vectors.astype(jnp.float32)), axis=2) * (
        0.5 * scaling * scaling
    )
    return key_dash - key_diag[:, :, None]


def key_terms(key_expo, key_peak, values):
    key_phi = jnp.exp(key_expo - key_peak[None, :, None]).astype(jnp.bfloat16)
    key_state = jnp.einsum("thm,the->hme", key_phi, values, preferred_element_type=jnp.float32)
    key_mass = jnp.sum(key_phi, axis=0, dtype=jnp.float32)
    return (key_state, key_mass)


def partial_output(query_dash, query_peak, state_half, key_mass):
    query_phi = jnp.exp(query_dash - query_peak[:, :, None]).astype(jnp.bfloat16)
    numerator = jnp.einsum(
        "thm,hme->the", query_phi, state_half, preferred_element_type=jnp.float32
    )
    denominator = jnp.einsum(
        "thm,hm->th", query_phi.astype(jnp.float32), key_mass, precision=lax.Precision.HIGHEST
    )
    return (numerator, denominator)


def shards(queries, key_vectors, values, projections):
    scaling = E ** (-0.25)
    directions = lax.all_to_all(projections, "feat", split_axis=0, concat_axis=1, tiled=True)
    head_share = queries.shape[1] // lax.axis_size("feat")
    start_head = lax.axis_index("feat") * head_share
    own_queries = lax.dynamic_slice_in_dim(queries, start_head, head_share, 1)
    own_keys = lax.dynamic_slice_in_dim(key_vectors, start_head, head_share, 1)
    own_values = lax.dynamic_slice_in_dim(values, start_head, head_share, 1)
    key_expo = key_exponents(own_keys, directions, scaling)
    key_peak = lax.pmax(jnp.max(key_expo, axis=(0, 2)), "seq")
    key_state, key_mass = key_terms(key_expo, key_peak, own_values)
    key_state, key_mass = lax.psum((key_state, key_mass), "seq")
    state_half = key_state.astype(jnp.bfloat16)
    query_dash = (
        jnp.einsum("the,hme->thm", own_queries, directions, preferred_element_type=jnp.float32)
        * scaling
    )
    numerator, denominator = partial_output(
        query_dash, jnp.max(query_dash, axis=2), state_half, key_mass
    )
    return (numerator / denominator[:, :, None]).astype(jnp.bfloat16)


def solution(mesh):
    placed = (
        P("seq", None, None),
        P("seq", None, None),
        P("seq", None, None),
        P(None, "feat", None),
    )
    return jax.shard_map(
        shards, mesh=mesh, in_specs=placed, out_specs=P("seq", "feat", None), check_vma=False
    )
```

profile of v0, /device:TPU:0, one launch (start us, length us, event | category | flops | bytes accessed | tf_op | source)
XLA Modules:
  0.0 290.5 jit_solution(13360563966676854355)
XLA Ops:
  0.0 6.4 %all-to-all-start = ((bf16[16,512,128]{2,1,0:T(8,128)(2,1)}), bf16[16,512,128]{2,1,0:T(8,128)(2,1)S(1)}, u32[]{:S(2)}, u32[]{:S(2)}) async-start(bf16[16,512,128]{2,1,0:T(8,128)(2,1)} %param.7), calls=%async_computation | async-start | bytes 4194304 | tf_op jit(solution)/shard_map/all_to_all | solution.py:40
  6.4 2.1 constant_dynamic-slice_fusion.2
  8.4 2.8 constant_dynamic-slice_fusion.1
  11.2 2.1 constant_dynamic-slice_fusion
  13.3 0.4 multiply_reduce_fusion
  13.7 41.7 %all-to-all-done = bf16[16,512,128]{2,1,0:T(8,128)(2,1)S(1)} async-done(((bf16[16,512,128]{2,1,0:T(8,128)(2,1)}), bf16[16,512,128]{2,1,0:T(8,128)(2,1)S(1)}, u32[]{:S(2)}, u32[]{:S(2)}) %all-to-all-start) | async-done | bytes 2097184 | tf_op jit(solution)/shard_map/all_to_all | solution.py:40
  55.4 0.0 copy-start
  55.4 1.3 copy-done
  56.7 1.7 copy.6
  58.5 12.5 %fusion.2 = (f32[2]{0:T(128)S(1)}, f32[2,960,4096]{2,1,0:T(8,128)}) fusion(f32[960,2]{0,1:T(2,128)S(1)} %broadcast_multiply_fusion, bf16[2,4096,128]{2,1,0:T(8,128)(2,1)S(1)} %bitcast.42, bf16[960,2,128]{2,1,0:T(2,128)(2,1)S(1)} %constant_dynamic-slice_fusion.2), kind=kOutput, calls=%fused_computation.7 | convolution fusion | flops 2036858880 | bytes 34053640 | tf_op jit(solution)/shard_map/the,hme->thm/dot_general | solution.py:11
  71.0 0.0 copy-start.1
  71.0 10.2 %pmax.7 = f32[2]{0:T(128)S(1)} all-reduce(f32[2]{0:T(128)S(1)} %get-tuple-element.9), channel_id=1, replica_groups=mesh['seq'=4,'feat'=8] {'seq'}, use_global_device_ids=true, to_apply=%region_2.0 | all-reduce | flops 2 | bytes 16 | tf_op jit(solution)/shard_map/pmax | solution.py:47
  81.1 14.1 %convert_reduce_fusion = (f32[2,4096]{1,0:T(2,128)S(1)}, bf16[960,2,4096]{2,0,1:T(8,128)(2,1)S(1)}) fusion(f32[2]{0:T(128)S(1)} %pmax.7, f32[960,2]{0,1:T(2,128)S(1)} %broadcast_multiply_fusion, f32[2,960,4096]{2,1,0:T(8,128)} %get-tuple-element.10), kind=kLoop, calls=%fused_computation.5 | loop fusion | flops 47177728 | bytes 47226376 | tf_op jit(solution)/shard_map/reduce_sum | solution.py:23
  95.3 0.0 copy-done.1
  95.3 8.3 %fusion.25 = f32[2,4096,128]{2,1,0:T(8,128)} fusion(bf16[960,2,4096]{2,0,1:T(8,128)(2,1)S(1)} %get-tuple-element.8, bf16[960,2,128]{2,1,0:T(2,128)(2,1)S(1)} %copy-done.1), kind=kOutput, calls=%fused_computation.17 | convolution fusion | flops 2013265920 | bytes 20414464 | tf_op jit(solution)/shard_map/thm,the->hme/dot_general | solution.py:22
  103.6 12.4 %bitcast_reduce_fusion = (f32[960,2]{0,1:T(2,128)S(1)}, f32[2,960,4096]{2,1,0:T(8,128)}) fusion(bf16[2,4096,128]{2,1,0:T(8,128)(2,1)S(1)} %bitcast.43, bf16[960,2,128]{2,1,0:T(2,128)(2,1)S(1)} %constant_dynamic-slice_fusion), kind=kOutput, calls=%fused_computation.1 | convolution fusion | flops 2028992640 | bytes 34053632 | tf_op jit(solution)/shard_map/the,hme->thm/dot_general | solution.py:52
  116.0 142.1 %all-reduce.2 = (bf16[2,4096,128]{2,1,0:T(8,128)(2,1)S(1)}, f32[2,4096]{1,0:T(2,128)S(1)}) all-reduce(f32[2,4096,128]{2,1,0:T(8,128)} %fusion.25, f32[2,4096]{1,0:T(2,128)S(1)} %get-tuple-element.7), channel_id=1, replica_groups=mesh['seq'=4,'feat'=8] {'seq'}, use_global_device_ids=true, to_apply=%region_3.0 | all-reduce | flops 1056768 | bytes 6356992 | tf_op jit(solution)/shard_map/psum | solution.py:49
  258.1 18.6 %fusion.3 = f32[2,1,960]{2,1,0:T(1,128)S(1)} fusion(f32[2,960,4096]{2,1,0:T(8,128)} %get-tuple-element.12, f32[960,2]{0,1:T(2,128)S(1)} %get-tuple-element.11, f32[2,4096,1]{1,0,2:T(2,128)S(1)} %bitcast.45), kind=kOutput, calls=%fused_computation.8 | convolution fusion | flops 117964800 | bytes 31505408 | tf_op jit(solution)/shard_map/thm,hm->th/dot_general | solution.py:32
  276.7 12.5 %fusion.18 = bf16[960,2,128]{2,0,1:T(8,128)(2,1)S(1)} fusion(bf16[2,4096,128]{2,1,0:T(8,128)(2,1)S(1)} %get-tuple-element.5, f32[2,960,4096]{2,1,0:T(8,128)} %get-tuple-element.12, f32[960,2]{0,1:T(2,128)S(1)} %get-tuple-element.11, f32[960,2]{0,1:T(2,128)S(1)} %bitcast.46), kind=kOutput, calls=%fused_computation.13 | convolution fusion | flops 2037350400 | bytes 34061312 | tf_op jit(solution)/shard_map/thm,hme->the/dot_general | solution.py:29
  289.2 1.3 copy.8
  (2 shorter events, 0.0 us)
Async XLA Ops:
  0.0 55.4 %all-to-all-start = ((bf16[16,512,128]{2,1,0:T(8,128)(2,1)}), bf16[16,512,128]{2,1,0:T(8,128)(2,1)S(1)}, u32[]{:S(2)}, u32[]{:S(2)}) async-start(bf16[16,512,128]{2,1,0:T(8,128)(2,1)} %param.7), calls=%async_computation | async-start | bytes 4194304 | tf_op jit(solution)/shard_map/all_to_all | solution.py:40
  55.4 1.4 copy-start
  71.0 24.3 %copy-start.1 = (bf16[960,2,128]{2,1,0:T(2,128)(2,1)S(1)}, bf16[960,2,128]{2,1,0:T(2,128)(2,1)}, u32[]{:S(2)}) copy-start(bf16[960,2,128]{2,1,0:T(2,128)(2,1)} %constant_dynamic-slice_fusion.1) | copy-start | bytes 1474564
where the time goes:
time: 291 us
  blocking collectives  152 us (52%)
  matrix products  64.3 us (22%)
  waiting for transfers between devices  41.7 us (14%)
  other arithmetic  14.5 us (5%)
  local copies, waits for them, and re-layouts  11.3 us (4%)
  starting transfers between devices  6.35 us (2%)
    psum x1, blocking collectives, shards(): key_state, key_mass = lax.psum((key_state, key_mass), 'seq')  142 us
    all_to_all x1, waiting for transfers between devices, shards(): lax.all_to_all(projections, 'feat', split_axis=0, concat_axis=1, tiled=True)  41.7 us
    dot_general x1, matrix products, partial_output(): jnp.einsum('thm,hm->th', query_phi.astype(jnp.float32), key_mass, precisi...  18.6 us
    reduce_sum x1, other arithmetic, key_terms(): key_mass = jnp.sum(key_phi, axis=0, dtype=jnp.float32)  14.1 us
    dot_general x1, matrix products, partial_output(): jnp.einsum('thm,hme->the', query_phi, state_half, preferred_element_type=...  12.5 us
    dot_general x1, matrix products, key_exponents(): jnp.einsum('the,hme->thm', key_vectors, directions, preferred_element_typ...  12.5 us
    dot_general x1, matrix products, shards(): jnp.einsum('the,hme->thm', own_queries, directions, preferred_element_typ...  12.4 us
    pmax x1, blocking collectives, shards(): key_peak = lax.pmax(jnp.max(key_expo, axis=(0, 2)), 'seq')  10.2 us
  transfers between devices with their start and end apart: 1, of which 1 were waited for; matrix products, arithmetic and copies ran while one was open for 3% of the time, Pallas kernels for 0%

commit v1 on v0

--- a/solution.py
+++ b/solution.py
@@ -37,7 +37,10 @@
 
 def shards(queries, key_vectors, values, projections):
     scaling = E ** (-0.25)
-    directions = lax.all_to_all(projections, "feat", split_axis=0, concat_axis=1, tiled=True)
+    peers = lax.axis_size("feat")
+    tiles = jnp.stack(jnp.split(projections, peers, axis=0), axis=0)
+    tiles = lax.all_to_all(tiles, "feat", split_axis=0, concat_axis=0)
+    directions = jnp.concatenate(tiles, axis=1)
     head_share = queries.shape[1] // lax.axis_size("feat")
     start_head = lax.axis_index("feat") * head_share
     own_queries = lax.dynamic_slice_in_dim(queries, start_head, head_share, 1)

time: 291 us -> 305 us (1.048)
  local copies, waits for them, and re-layouts: 11.3 us -> 24.7 us
    unnamed x4 -> x11, local copies, waits for them, and re-layouts: 1.35 us -> 13.1 us
  transfers between devices with their start and end apart: 1 -> 1, of which waited for: 1 -> 1; matrix products, arithmetic and copies ran while one was open for 3% -> 2% of each run, Pallas kernels for 0% -> 0%
where the time goes in v1:
time: 305 us; the launch traced here: 304 us
  blocking collectives  152 us (50%)
  matrix products  64.3 us (21%)
  waiting for transfers between devices  41.7 us (14%)
  local copies, waits for them, and re-layouts  24.7 us (8%)
  other arithmetic  14.5 us (5%)
  starting transfers between devices  6.35 us (2%)
    psum x1, blocking collectives, shards(): key_state, key_mass = lax.psum((key_state, key_mass), 'seq')  142 us
    all_to_all x1, waiting for transfers between devices, shards(): tiles = lax.all_to_all(tiles, 'feat', split_axis=0, concat_axis=0)  41.7 us
    dot_general x1, matrix products, partial_output(): jnp.einsum('thm,hm->th', query_phi.astype(jnp.float32), key_mass, precisi...  18.6 us
    reduce_sum x1, other arithmetic, key_terms(): key_mass = jnp.sum(key_phi, axis=0, dtype=jnp.float32)  14.2 us
    unnamed x11, local copies, waits for them, and re-layouts  13.1 us
    dot_general x1, matrix products, partial_output(): jnp.einsum('thm,hme->the', query_phi, state_half, preferred_element_type=...  12.5 us
    dot_general x1, matrix products, key_exponents(): jnp.einsum('the,hme->thm', key_vectors, directions, preferred_element_typ...  12.5 us
    dot_general x1, matrix products, shards(): jnp.einsum('the,hme->thm', own_queries, directions, preferred_element_typ...  12.4 us
  transfers between devices with their start and end apart: 1, of which 1 were waited for; matrix products, arithmetic and copies ran while one was open for 2% of the time, Pallas kernels for 0%

profile of v1, /device:TPU:0, one launch (start us, length us, event | category | flops | bytes accessed | tf_op | source)
XLA Modules:
  0.0 303.8 jit_solution(8207512203763111166)
XLA Ops:
  0.0 1.7 bitcast_dynamic-update-slice_fusion.7
  1.7 1.7 bitcast_dynamic-update-slice_fusion.6
  3.3 1.7 bitcast_dynamic-update-slice_fusion.5
  5.0 1.7 bitcast_dynamic-update-slice_fusion.4
  6.7 1.7 bitcast_dynamic-update-slice_fusion.3
  8.4 1.7 bitcast_dynamic-update-slice_fusion.2
  10.0 1.7 bitcast_dynamic-update-slice_fusion.1
  11.7 1.7 bitcast_dynamic-update-slice_fusion
  13.4 6.4 %all-to-all-start = ((bf16[8,2,512,128]{3,2,1,0:T(8,128)(2,1)}), bf16[8,2,512,128]{3,2,1,0:T(8,128)(2,1)S(1)}, u32[]{:S(2)}, u32[]{:S(2)}) async-start(bf16[8,2,512,128]{3,2,1,0:T(8,128)(2,1)} %bitcast_dynamic-update-slice_fusion), calls=%async_computation | async-start | bytes 4194304 | tf_op jit(solution)/shard_map/all_to_all | solution.py:42
  19.7 2.1 constant_dynamic-slice_fusion.2
  21.8 2.8 constant_dynamic-slice_fusion.1
  24.6 2.1 constant_dynamic-slice_fusion
  27.1 41.7 %all-to-all-done = bf16[8,2,512,128]{3,2,1,0:T(8,128)(2,1)S(1)} async-done(((bf16[8,2,512,128]{3,2,1,0:T(8,128)(2,1)}), bf16[8,2,512,128]{3,2,1,0:T(8,128)(2,1)S(1)}, u32[]{:S(2)}, u32[]{:S(2)}) %all-to-all-start) | async-done | bytes 2097184 | tf_op jit(solution)/shard_map/all_to_all | solution.py:42
  68.8 1.3 copy-done
  70.1 1.7 copy.5
  71.9 12.5 %fusion.2 = (f32[2]{0:T(128)S(1)}, f32[2,4096,960]{1,2,0:T(8,128)}) fusion(f32[960,2]{0,1:T(2,128)S(1)} %broadcast_multiply_fusion, bf16[2,4096,128]{2,1,0:T(8,128)(2,1)S(1)} %bitcast.56, bf16[960,2,128]{2,1,0:T(2,128)(2,1)S(1)} %constant_dynamic-slice_fusion.2), kind=kOutput, calls=%fused_computation.7 | convolution fusion | flops 2036858880 | bytes 34053640 | tf_op jit(solution)/shard_map/the,hme->thm/dot_general | solution.py:11
  84.3 10.1 %pmax.7 = f32[2]{0:T(128)S(1)} all-reduce(f32[2]{0:T(128)S(1)} %get-tuple-element.9), channel_id=1, replica_groups=mesh['seq'=4,'feat'=8] {'seq'}, use_global_device_ids=true, to_apply=%region_2.0 | all-reduce | flops 2 | bytes 16 | tf_op jit(solution)/shard_map/pmax | solution.py:50
  94.4 14.2 %convert_reduce_fusion = (f32[2,4096]{1,0:T(2,128)S(1)}, bf16[960,2,4096]{2,0,1:T(8,128)(2,1)S(1)}) fusion(f32[2]{0:T(128)S(1)} %pmax.7, f32[960,2]{0,1:T(2,128)S(1)} %broadcast_multiply_fusion, f32[2,4096,960]{1,2,0:T(8,128)} %get-tuple-element.10), kind=kLoop, calls=%fused_computation.5 | loop fusion | flops 47177728 | bytes 47226376 | tf_op jit(solution)/shard_map/reduce_sum | solution.py:23
  108.6 8.3 %fusion.25 = f32[2,4096,128]{2,1,0:T(8,128)} fusion(bf16[960,2,4096]{2,0,1:T(8,128)(2,1)S(1)} %get-tuple-element.8, bf16[960,2,128]{2,1,0:T(2,128)(2,1)S(1)} %copy-done.1), kind=kOutput, calls=%fused_computation.17 | convolution fusion | flops 2013265920 | bytes 20414464 | tf_op jit(solution)/shard_map/thm,the->hme/dot_general | solution.py:22
  116.9 12.4 %bitcast_reduce_fusion = (f32[960,2]{0,1:T(2,128)S(1)}, f32[2,4096,960]{1,2,0:T(8,128)}) fusion(bf16[2,4096,128]{2,1,0:T(8,128)(2,1)S(1)} %bitcast.57, bf16[960,2,128]{2,1,0:T(2,128)(2,1)S(1)} %constant_dynamic-slice_fusion), kind=kOutput, calls=%fused_computation.1 | convolution fusion | flops 2028992640 | bytes 34053632 | tf_op jit(solution)/shard_map/the,hme->thm/dot_general | solution.py:55
  129.3 142.1 %all-reduce.2 = (bf16[2,4096,128]{2,1,0:T(8,128)(2,1)S(1)}, f32[2,4096]{1,0:T(2,128)S(1)}) all-reduce(f32[2,4096,128]{2,1,0:T(8,128)} %fusion.25, f32[2,4096]{1,0:T(2,128)S(1)} %get-tuple-element.7), channel_id=1, replica_groups=mesh['seq'=4,'feat'=8] {'seq'}, use_global_device_ids=true, to_apply=%region_3.0 | all-reduce | flops 1056768 | bytes 6356992 | tf_op jit(solution)/shard_map/psum | solution.py:52
  271.4 18.6 %fusion.3 = f32[2,1,960]{2,1,0:T(1,128)S(1)} fusion(f32[2,4096,960]{1,2,0:T(8,128)} %get-tuple-element.12, f32[960,2]{0,1:T(2,128)S(1)} %get-tuple-element.11, f32[2,4096,1]{1,0,2:T(2,128)S(1)} %bitcast.59), kind=kOutput, calls=%fused_computation.8 | convolution fusion | flops 117964800 | bytes 31505408 | tf_op jit(solution)/shard_map/thm,hm->th/dot_general | solution.py:32
  290.0 12.5 %fusion.18 = bf16[960,2,128]{2,0,1:T(8,128)(2,1)S(1)} fusion(bf16[2,4096,128]{2,1,0:T(8,128)(2,1)S(1)} %get-tuple-element.5, f32[2,4096,960]{1,2,0:T(8,128)} %get-tuple-element.12, f32[960,2]{0,1:T(2,128)S(1)} %get-tuple-element.11, f32[960,2]{0,1:T(2,128)S(1)} %bitcast.60), kind=kOutput, calls=%fused_computation.13 | convolution fusion | flops 2037350400 | bytes 34061312 | tf_op jit(solution)/shard_map/thm,hme->the/dot_general | solution.py:29
  302.5 1.3 copy.8
  (6 shorter events, 0.4 us)
Async XLA Ops:
  13.4 55.4 %all-to-all-start = ((bf16[8,2,512,128]{3,2,1,0:T(8,128)(2,1)}), bf16[8,2,512,128]{3,2,1,0:T(8,128)(2,1)S(1)}, u32[]{:S(2)}, u32[]{:S(2)}) async-start(bf16[8,2,512,128]{3,2,1,0:T(8,128)(2,1)} %bitcast_dynamic-update-slice_fusion), calls=%async_computation | async-start | bytes 4194304 | tf_op jit(solution)/shard_map/all_to_all | solution.py:42
  68.8 1.4 copy-start
  94.4 14.2 %copy-start.1 = (bf16[960,2,128]{2,1,0:T(2,128)(2,1)S(1)}, bf16[960,2,128]{2,1,0:T(2,128)(2,1)}, u32[]{:S(2)}) copy-start(bf16[960,2,128]{2,1,0:T(2,128)(2,1)} %constant_dynamic-slice_fusion.1) | copy-start | bytes 1474564
